TPU v7x, 32 devices: a whole 2x2x4 slice. The times are simulated.
32 devices in a mesh: gx: 8 (over y, x, core), pa: 4 (over z).
Axes of the slice: x: 2, y: 2, z: 4, core: 2. Of those that a mesh axis runs over, the one named last changes fastest.
Arguments:
- block_inverses: float32 [32, 32, 128, 128], P('gx', 'pa'), parts along dimension 1, may hold values from -0.25 to 1.07, as said below
- residual: float32 [32, 32, 128], P('gx', 'pa'), parts along dimension 1, may hold values from -0.3 to 0.3
- material: int32 [32, 32, 128], P('gx', 'pa'), parts along dimension 1, may hold values from 0 to 3
- fin_mask: int32 [32, 32, 128], P('gx', 'pa'), parts along dimension 1, may hold values 0 or 1
- phase_mask: int32 [32, 32, 128], P('gx', 'pa'), parts along dimension 1, may hold values 0 or 1
- k_table: float32 [4], replicated, may hold values from 0.95 to 1.05
Outputs:
- correction: float32 [32, 32, 128], P('gx', 'pa'), parts along dimension 1
- enthalpy_step: float32 [32, 32, 128], P('gx', 'pa'), parts along dimension 1
There are 4 independent parts, one for each index of `pa`. A program takes and returns all parts, laid end to end along the dimension named above; an argument that names none is the same for every part. Nothing has to cross between parts.
Inputs may be any that keep to these rules, and one draw needn't show every extreme that they name: Each block block_inverses[i, t] is a symmetric matrix.
All inputs are finite; a program needn't handle non-finite values. No bound on the sum of `fin_mask` or of `phase_mask` on one device may be relied on, other than what follows from the above.
Results may differ from a plain program's by a relative error of at most 0.0003.
Values sent between devices are 32-bit elements; how exact they have to be, the bound alone decides.
No kernel may reach another device: no remote copies, remote signals or barrier semaphores. Data moves between devices by JAX's collectives and lax.ppermute only.
A program may use at most 128 MiB of HBM per device.

v0:
```python
import jax
import jax.numpy as jnp
from jax import lax
from jax.sharding import PartitionSpec as P


def passed_along(block, axis, distance):
    devices = range(lax.axis_size(axis))
    route = [(i - distance, i) for i in devices if i - distance in devices]
    return lax.ppermute(block, axis, route)


def apply_block(pivot_entries, vector):
    return jnp.einsum("tab,tb->ta", pivot_entries, vector, precision=lax.Precision.HIGHEST)


def apply_transposed(pivot_entries, vector):
    return jnp.einsum("tba,tb->ta", pivot_entries, vector, precision=lax.Precision.HIGHEST)


def forward_pass(block_inverses, residual, face_cond, entering):
    state_vec = entering
    results = []
    for line_position in range(block_inverses.shape[0]):
        state_vec = apply_block(
            block_inverses[line_position],
            residual[line_position] + face_cond[line_position] * state_vec,
        )
        results.append(state_vec)
    return jnp.stack(results)


def backward_pass(block_inverses, forward_vals, face_cond, arriving):
    carried = arriving
    results = [None] * block_inverses.shape[0]
    for line_position in reversed(range(block_inverses.shape[0])):
        solved = forward_vals[line_position] + apply_block(block_inverses[line_position], carried)
        results[line_position] = solved
        carried = face_cond[line_position] * solved
    return (jnp.stack(results), carried)


def on_device(block_inverses, residual, material, fin_mask, phase_mask, k_table):
    block_count, tile_count, cell_count = residual.shape
    material_codes = jnp.arange(k_table.shape[0], dtype=jnp.int32)
    conduct = jnp.sum(
        jnp.where(material[..., None] == material_codes, k_table, jnp.zeros_like(k_table)), axis=-1
    )
    before = passed_along(conduct[block_count - 1], "gx", 1)
    earlier = jnp.concatenate([before[None], conduct[: block_count - 1]], axis=0)
    face_cond = (
        2.0 * conduct * earlier / (conduct + earlier) * (0.9 + 0.1 * fin_mask.astype(jnp.float32))
    )
    zero_vector = jnp.zeros((tile_count, cell_count), jnp.float32)
    scaled_rows = block_inverses * face_cond[:, :, None, :]
    matrix_product = scaled_rows[0]
    for line_position in range(1, block_count):
        matrix_product = jnp.einsum(
            "hzp,hpn->hzn",
            scaled_rows[line_position],
            matrix_product,
            precision=lax.Precision.HIGHEST,
        )
    local_vals = forward_pass(block_inverses, residual, face_cond, zero_vector)
    tail_vec = local_vals[block_count - 1]
    all_maps, all_tails = (
        lax.all_gather(matrix_product[None], "gx", axis=0, tiled=True),
        lax.all_gather(tail_vec[None], "gx", axis=0, tiled=True),
    )
    own_index = lax.axis_index("gx")
    processor_total = all_maps.shape[0]

    def fold_forward(line_position, state_vec):
        moved = apply_block(all_maps[line_position], state_vec) + all_tails[line_position]
        return jnp.where(line_position < own_index, moved, state_vec)

    entering = lax.fori_loop(0, processor_total, fold_forward, zero_vector, unroll=8)
    forward_vals = forward_pass(block_inverses, residual, face_cond, entering)
    _, leaving = backward_pass(block_inverses, forward_vals, face_cond, zero_vector)
    all_leaving = lax.all_gather(leaving[None], "gx", axis=0, tiled=True)

    def backward_accumulate(offset, state_vec):
        line_position = processor_total - 1 - offset
        moved = apply_transposed(all_maps[line_position], state_vec) + all_leaving[line_position]
        return jnp.where(line_position > own_index, moved, state_vec)

    arriving = lax.fori_loop(0, processor_total, backward_accumulate, zero_vector, unroll=8)
    correction, _ = backward_pass(block_inverses, forward_vals, face_cond, arriving)
    enthalpy_step = correction * (1.0 + 2.0 * phase_mask.astype(jnp.float32))
    return (correction, enthalpy_step)


def solution(mesh):
    return jax.shard_map(
        on_device,
        mesh=mesh,
        in_specs=(
            P("gx", "pa", None, None),
            P("gx", "pa", None),
            P("gx", "pa", None),
            P("gx", "pa", None),
            P("gx", "pa", None),
            P(),
        ),
        out_specs=(P("gx", "pa", None), P("gx", "pa", None)),
        check_vma=False,
    )
```

profile of v0, /device:TPU:0, one launch (start us, length us, event | category | flops | bytes accessed | tf_op | source)
XLA Modules:
  0.0 100.5 jit_solution(474527091113292094)
XLA Ops:
  8.0 2.3 %collective-permute-start = (f32[8,128]{1,0:T(8,128)S(1)}, f32[8,128]{1,0:T(8,128)S(1)}, u32[]{:S(2)}, u32[]{:S(2)}) collective-permute-start(f32[8,128]{1,0:T(8,128)S(1)} %slice_bitcast_fusion.12), channel_id=1, source_target_pairs={{0,4},{4,8},{8,12},{12,16},{16,20},{20,24},{24,28},{1,5},{5,9},{9,... | collective-permute-start | bytes 12296 | tf_op jit(solution)/shard_map/ppermute | solution.py:10
  11.9 1.9 %broadcast_multiply_fusion = f32[4,8,128,128]{3,2,1,0:T(8,128)S(1)} fusion(f32[4,8,128,128]{3,2,1,0:T(8,128)} %param.6, f32[4,8,128]{2,1,0:T(8,128)S(1)} %add_multiply_fusion.1), kind=kLoop, calls=%fused_computation | loop fusion | flops 524288 | bytes 4210688 | tf_op jit(solution)/shard_map/mul | solution.py:55
  15.2 1.5 %fusion.2 = f32[8,128,128]{2,1,0:T(8,128)} fusion(f32[8,128,128]{2,1,0:T(8,128)S(1)} %fusion.1, f32[4,8,128,128]{3,2,1,0:T(8,128)S(1)} %broadcast_multiply_fusion), kind=kOutput, calls=%fused_computation.7 | convolution fusion | flops 201326592 | bytes 1572864 | tf_op jit(solution)/shard_map/hzp,hpn->hzn/dot_general | solution.py:58
  17.7 0.9 fusion.33
  18.6 0.9 fusion.25
  19.6 1.0 fusion.17
  21.5 13.4 %all-gather.1 = f32[64,128]{1,0:T(8,128)S(1)} all-gather(f32[8,128]{1,0:T(8,128)S(1)} %bitcast.349), channel_id=3, replica_groups=mesh['gx'=8,'pa'=4] {'gx'}, dimensions={0}, use_global_device_ids=true | all-gather | bytes 36864 | tf_op jit(solution)/shard_map/all_gather | solution.py:68
  34.8 23.2 %all-gather.5.cloned.1.call-done = f32[64,128,128]{2,1,0:T(8,128)} async-done(((f32[8,128,128]{2,1,0:T(8,128)}), f32[64,128,128]{2,1,0:T(8,128)}) %all-gather.5.cloned.1.call-update) | async-done | bytes 4194320 | tf_op jit(solution)/shard_map/all_gather | solution.py:67
  58.0 2.1 %fusion.72 = f32[8,1,128]{2,1,0:T(1,128)S(1)} fusion(f32[64,128,128]{2,1,0:T(8,128)} %all-gather.5.cloned.1.call-done, f32[8,128,1]{1,2,0:T(1,128)S(1)} %bitcast.312), kind=kOutput, calls=%fused_computation.119 | convolution fusion | flops 1572864 | bytes 4202496 | tf_op jit(solution)/shard_map/eval_jaxpr/tab,tb->ta/dot_general | solution.py:14
  60.1 2.0 %fusion.73 = f32[8,1,128]{2,1,0:T(1,128)S(1)} fusion(f32[64,128,128]{2,1,0:T(8,128)} %all-gather.5.cloned.1.call-done, f32[8,128,1]{1,2,0:T(1,128)S(1)} %bitcast.326), kind=kOutput, calls=%fused_computation.120 | convolution fusion | flops 1572864 | bytes 4202496 | tf_op jit(solution)/shard_map/eval_jaxpr/tab,tb->ta/dot_general | solution.py:14
  62.1 2.0 %fusion.74 = f32[8,1,128]{2,1,0:T(1,128)S(1)} fusion(f32[64,128,128]{2,1,0:T(8,128)} %all-gather.5.cloned.1.call-done, f32[8,128,1]{1,2,0:T(1,128)S(1)} %bitcast.329), kind=kOutput, calls=%fused_computation.121 | convolution fusion | flops 1572864 | bytes 4202496 | tf_op jit(solution)/shard_map/eval_jaxpr/tab,tb->ta/dot_general | solution.py:14
  65.0 0.9 fusion.76
  68.8 0.9 fusion.31
  69.7 0.9 fusion.23
  70.7 0.9 fusion.15
  71.6 0.9 fusion.7
  72.6 0.9 fusion.13
  73.5 0.9 fusion.21
  74.5 0.9 fusion.29
  75.4 9.2 %all-gather.2 = f32[64,128]{1,0:T(8,128)S(1)} all-gather(f32[8,128]{1,0:T(8,128)S(1)} %add_multiply_fusion.2), channel_id=4, replica_groups=mesh['gx'=8,'pa'=4] {'gx'}, dimensions={0}, use_global_device_ids=true | all-gather | bytes 36864 | tf_op jit(solution)/shard_map/all_gather | solution.py:80
  89.2 0.9 fusion.3
  90.2 0.9 fusion.11
  91.1 0.9 fusion.19
  92.0 0.9 fusion.27
  (64 shorter events, 14.6 us)
Async XLA Ops:
  7.2 50.9 %all-gather.5.cloned.1.call-start = ((), (), s32[]{:S(2)}) async-start(), calls=%async_computation | async-start | bytes 4718592 | tf_op jit(solution)/shard_map/all_gather | solution.py:67
  8.0 3.2 %collective-permute-start = (f32[8,128]{1,0:T(8,128)S(1)}, f32[8,128]{1,0:T(8,128)S(1)}, u32[]{:S(2)}, u32[]{:S(2)}) collective-permute-start(f32[8,128]{1,0:T(8,128)S(1)} %slice_bitcast_fusion.12), channel_id=1, source_target_pairs={{0,4},{4,8},{8,12},{12,16},{16,20},{20,24},{24,28},{1,5},{5,9},{9,... | collective-permute-start | bytes 12296 | tf_op jit(solution)/shard_map/ppermute | solution.py:10
  11.9 4.8 %copy-start.1 = (f32[4,8,128,128]{3,2,1,0:T(8,128)S(1)}, f32[4,8,128,128]{3,2,1,0:T(8,128)}, u32[]{:S(2)}) copy-start(f32[4,8,128,128]{3,2,1,0:T(8,128)} %param.6) | copy-start | bytes 6291460
  11.9 5.8 %copy-start.2 = (f32[4,8,128]{2,1,0:T(8,128)S(1)}, f32[4,8,128]{2,1,0:T(8,128)}, u32[]{:S(2)}) copy-start(f32[4,8,128]{2,1,0:T(8,128)} %param.7) | copy-start | bytes 49156
  58.0 6.1 %copy-start = (f32[64,128,128]{2,1,0:T(8,128)S(1)}, f32[64,128,128]{2,1,0:T(8,128)}, u32[]{:S(2)}) copy-start(f32[64,128,128]{2,1,0:T(8,128)} %all-gather.5.cloned.1.call-done) | copy-start | bytes 12582916
  86.9 6.1 %copy-start.3 = (s32[4,8,128]{2,1,0:T(8,128)S(1)}, s32[4,8,128]{2,1,0:T(8,128)}, u32[]{:S(2)}) copy-start(s32[4,8,128]{2,1,0:T(8,128)} %param.10) | copy-start | bytes 49156
Sparse Core Ops, SparseCore 0:
  16.8 41.1 all-gather.4
where the time goes:
time: 101 us; the launch traced here: 100 us
  matrix products  32.9 us (33%)
  waiting for transfers between devices  24 us (24%)
  blocking collectives  22.6 us (22%)
  between operations  14.2 us (14%)
  other arithmetic  4.31 us (4%)
  starting transfers between devices  2.38 us (2%)
    dot_general x24, matrix products, apply_block(): jnp.einsum('tab,tb->ta', pivot_entries, vector, precision=lax.Precision.H...  25.7 us
    all_gather x1, waiting for transfers between devices, on_device(): lax.all_gather(matrix_product[None], 'gx', axis=0, tiled=True)  23.2 us
    all_gather x1, blocking collectives, on_device(): lax.all_gather(tail_vec[None], 'gx', axis=0, tiled=True)  13.4 us
    all_gather x1, blocking collectives, on_device(): all_leaving = lax.all_gather(leaving[None], 'gx', axis=0, tiled=True)  9.25 us
    dot_general x8, matrix products, apply_transposed(): jnp.einsum('tba,tb->ta', pivot_entries, vector, precision=lax.Precision.H...  4.48 us
    dot_general x3, matrix products, on_device(): jnp.einsum('hzp,hpn->hzn', scaled_rows[line_position], matrix_product, pr...  2.81 us
    ppermute x1, starting transfers between devices, passed_along(): return lax.ppermute(block, axis, route)  2.35 us
  transfers between devices with their start and end apart: 2, of which 2 were waited for; matrix products, arithmetic and copies ran while one was open for 5% of the time, Pallas kernels for 0%

commit v1 on v0

--- a/solution.py
+++ b/solution.py
@@ -1,7 +1,27 @@
+import functools
 import jax
 import jax.numpy as jnp
 from jax import lax
 from jax.sharding import PartitionSpec as P
+
+
+def widths_update(mine_x, axis_no):
+    steps_seen = []
+    degree = jax.lax.axis_size("gx")
+    for nth in range(degree):
+        steps_seen.append((nth, (nth + 1) % degree))
+    last = [None] * degree
+    last[degree - 1] = mine_x
+    for jj in range(degree - 2, -1, -1):
+        last[jj] = jax.lax.ppermute(last[jj + 1], "gx", steps_seen)
+    odd = jnp.concatenate(last, axis=axis_no)
+    frame_out = jax.lax.axis_index("gx")
+    tile_out = (frame_out + 1) * mine_x.shape[axis_no]
+    newest = jnp.roll(odd, tile_out, axis=axis_no)
+    return newest
+
+
+unit_define = functools.partial(widths_update, axis_no=0)
 
 
 def passed_along(block, axis, distance):
@@ -77,7 +97,7 @@
     entering = lax.fori_loop(0, processor_total, fold_forward, zero_vector, unroll=8)
     forward_vals = forward_pass(block_inverses, residual, face_cond, entering)
     _, leaving = backward_pass(block_inverses, forward_vals, face_cond, zero_vector)
-    all_leaving = lax.all_gather(leaving[None], "gx", axis=0, tiled=True)
+    all_leaving = unit_define(leaving[None])
 
     def backward_accumulate(offset, state_vec):
         line_position = processor_total - 1 - offset

time: 101 us -> 121 us (1.20)
  waiting for transfers between devices: 24 us -> 49.7 us
  blocking collectives: 22.6 us -> 13.4 us
  matrix products: 32.9 us -> 36 us
    ppermute x0 -> x7, waiting for transfers between devices: none -> 25.7 us  [widths_update(): last[jj] = jax.lax.ppermute(last[jj + 1], 'gx', steps_seen)]
    all_gather x1 -> x0, blocking collectives: 9.25 us -> none  [on_device(): all_leaving = lax.all_gather(leaving[None], 'gx', axis=0, tiled=True)]
    dot_general x8, matrix products: 4.48 us -> 7.57 us  [apply_transposed(): jnp.einsum('tba,tb->ta', pivot_entries, vector, precision=lax.Precision.H...]
  transfers between devices with their start and end apart: 2 -> 9, of which waited for: 2 -> 9; matrix products, arithmetic and copies ran while one was open for 5% -> 5% of each run, Pallas kernels for 0% -> 0%
where the time goes in v1:
time: 121 us; the launch traced here: 120 us
  waiting for transfers between devices  49.7 us (41%)
  matrix products  36 us (30%)
  between operations  14.3 us (12%)
  blocking collectives  13.4 us (11%)
  other arithmetic  4.33 us (4%)
  starting transfers between devices  2.69 us (2%)
    dot_general x24, matrix products, apply_block(): jnp.einsum('tab,tb->ta', pivot_entries, vector, precision=lax.Precision.H...  25.7 us
    ppermute x7, waiting for transfers between devices, widths_update(): last[jj] = jax.lax.ppermute(last[jj + 1], 'gx', steps_seen)  25.7 us
    all_gather x1, waiting for transfers between devices, on_device(): lax.all_gather(matrix_product[None], 'gx', axis=0, tiled=True)  23.2 us
    all_gather x1, blocking collectives, on_device(): lax.all_gather(tail_vec[None], 'gx', axis=0, tiled=True)  13.4 us
    dot_general x8, matrix products, apply_transposed(): jnp.einsum('tba,tb->ta', pivot_entries, vector, precision=lax.Precision.H...  7.57 us
    dot_general x3, matrix products, on_device(): jnp.einsum('hzp,hpn->hzn', scaled_rows[line_position], matrix_product, pr...  2.79 us
  transfers between devices with their start and end apart: 9, of which 9 were waited for; matrix products, arithmetic and copies ran while one was open for 5% of the time, Pallas kernels for 0%

profile of v1, /device:TPU:0, one launch (start us, length us, event | category | flops | bytes accessed | tf_op | source)
XLA Modules:
  0.0 120.5 jit_solution(5838484401026664042)
XLA Ops:
  8.0 2.3 %collective-permute-start = (f32[8,128]{1,0:T(8,128)S(1)}, f32[8,128]{1,0:T(8,128)S(1)}, u32[]{:S(2)}, u32[]{:S(2)}) collective-permute-start(f32[8,128]{1,0:T(8,128)S(1)} %slice_bitcast_fusion.12), channel_id=1, source_target_pairs={{0,4},{4,8},{8,12},{12,16},{16,20},{20,24},{24,28},{1,5},{5,9},{9,... | collective-permute-start | bytes 12296 | tf_op jit(solution)/shard_map/ppermute | solution.py:30
  11.9 1.9 %broadcast_multiply_fusion = f32[4,8,128,128]{3,2,1,0:T(8,128)S(1)} fusion(f32[4,8,128,128]{3,2,1,0:T(8,128)} %param.6, f32[4,8,128]{2,1,0:T(8,128)S(1)} %add_multiply_fusion.1), kind=kLoop, calls=%fused_computation | loop fusion | flops 524288 | bytes 4210688 | tf_op jit(solution)/shard_map/mul | solution.py:75
  15.2 1.5 %fusion.2 = f32[8,128,128]{2,1,0:T(8,128)} fusion(f32[8,128,128]{2,1,0:T(8,128)S(1)} %fusion.1, f32[4,8,128,128]{3,2,1,0:T(8,128)S(1)} %broadcast_multiply_fusion), kind=kOutput, calls=%fused_computation.7 | convolution fusion | flops 201326592 | bytes 1572864 | tf_op jit(solution)/shard_map/hzp,hpn->hzn/dot_general | solution.py:78
  17.7 0.9 fusion.33
  18.6 0.9 fusion.25
  19.6 1.0 fusion.17
  21.4 13.4 %all-gather.1 = f32[64,128]{1,0:T(8,128)S(1)} all-gather(f32[8,128]{1,0:T(8,128)S(1)} %bitcast.406), channel_id=3, replica_groups=mesh['gx'=8,'pa'=4] {'gx'}, dimensions={0}, use_global_device_ids=true | all-gather | bytes 36864 | tf_op jit(solution)/shard_map/all_gather | solution.py:88
  34.8 23.2 %all-gather.4.cloned.1.call-done = f32[64,128,128]{2,1,0:T(8,128)} async-done(((f32[8,128,128]{2,1,0:T(8,128)}), f32[64,128,128]{2,1,0:T(8,128)}) %all-gather.4.cloned.1.call-update) | async-done | bytes 4194320 | tf_op jit(solution)/shard_map/all_gather | solution.py:87
  58.0 2.1 %fusion.80 = f32[8,1,128]{2,1,0:T(1,128)S(1)} fusion(f32[64,128,128]{2,1,0:T(8,128)} %all-gather.4.cloned.1.call-done, f32[8,128,1]{1,2,0:T(1,128)S(1)} %bitcast.362), kind=kOutput, calls=%fused_computation.143 | convolution fusion | flops 1572864 | bytes 4202496 | tf_op jit(solution)/shard_map/eval_jaxpr/tab,tb->ta/dot_general | solution.py:34
  60.1 2.0 %fusion.81 = f32[8,1,128]{2,1,0:T(1,128)S(1)} fusion(f32[64,128,128]{2,1,0:T(8,128)} %all-gather.4.cloned.1.call-done, f32[8,128,1]{1,2,0:T(1,128)S(1)} %bitcast.383), kind=kOutput, calls=%fused_computation.144 | convolution fusion | flops 1572864 | bytes 4202496 | tf_op jit(solution)/shard_map/eval_jaxpr/tab,tb->ta/dot_general | solution.py:34
  62.1 2.0 %fusion.82 = f32[8,1,128]{2,1,0:T(1,128)S(1)} fusion(f32[64,128,128]{2,1,0:T(8,128)} %all-gather.4.cloned.1.call-done, f32[8,128,1]{1,2,0:T(1,128)S(1)} %bitcast.384), kind=kOutput, calls=%fused_computation.145 | convolution fusion | flops 1572864 | bytes 4202496 | tf_op jit(solution)/shard_map/eval_jaxpr/tab,tb->ta/dot_general | solution.py:34
  68.8 0.9 fusion.31
  69.7 0.9 fusion.23
  70.7 0.9 fusion.15
  75.7 3.7 %collective-permute-done.1 = f32[1,8,128]{2,1,0:T(8,128)S(1)} collective-permute-done((f32[1,8,128]{2,1,0:T(8,128)S(1)}, f32[1,8,128]{2,1,0:T(8,128)S(1)}, u32[]{:S(2)}, u32[]{:S(2)}) %collective-permute-start.1) | collective-permute-done | bytes 4128 | tf_op jit(solution)/shard_map/ppermute | solution.py:16
  79.4 3.9 %collective-permute-done.2 = f32[1,8,128]{2,1,0:T(8,128)S(1)} collective-permute-done((f32[1,8,128]{2,1,0:T(8,128)S(1)}, f32[1,8,128]{2,1,0:T(8,128)S(1)}, u32[]{:S(2)}, u32[]{:S(2)}) %collective-permute-start.2) | collective-permute-done | bytes 4128 | tf_op jit(solution)/shard_map/ppermute | solution.py:16
  83.3 3.9 %collective-permute-done.3 = f32[1,8,128]{2,1,0:T(8,128)S(1)} collective-permute-done((f32[1,8,128]{2,1,0:T(8,128)S(1)}, f32[1,8,128]{2,1,0:T(8,128)S(1)}, u32[]{:S(2)}, u32[]{:S(2)}) %collective-permute-start.3) | collective-permute-done | bytes 4128 | tf_op jit(solution)/shard_map/ppermute | solution.py:16
  87.2 3.9 %collective-permute-done.4 = f32[1,8,128]{2,1,0:T(8,128)S(1)} collective-permute-done((f32[1,8,128]{2,1,0:T(8,128)S(1)}, f32[1,8,128]{2,1,0:T(8,128)S(1)}, u32[]{:S(2)}, u32[]{:S(2)}) %collective-permute-start.4) | collective-permute-done | bytes 4128 | tf_op jit(solution)/shard_map/ppermute | solution.py:16
  91.2 3.9 %collective-permute-done.5 = f32[1,8,128]{2,1,0:T(8,128)S(1)} collective-permute-done((f32[1,8,128]{2,1,0:T(8,128)S(1)}, f32[1,8,128]{2,1,0:T(8,128)S(1)}, u32[]{:S(2)}, u32[]{:S(2)}) %collective-permute-start.5) | collective-permute-done | bytes 4128 | tf_op jit(solution)/shard_map/ppermute | solution.py:16
  95.1 3.9 %collective-permute-done.6 = f32[1,8,128]{2,1,0:T(8,128)S(1)} collective-permute-done((f32[1,8,128]{2,1,0:T(8,128)S(1)}, f32[1,8,128]{2,1,0:T(8,128)S(1)}, u32[]{:S(2)}, u32[]{:S(2)}) %collective-permute-start.6) | collective-permute-done | bytes 4128 | tf_op jit(solution)/shard_map/ppermute | solution.py:16
  99.0 1.6 %fusion.88 = f32[8,1,128]{2,1,0:T(1,128)S(1)} fusion(f32[64,128,128]{2,1,0:T(8,128)} %all-gather.4.cloned.1.call-done, f32[8,128,1]{1,2,0:T(1,128)S(1)} %bitcast.363), kind=kOutput, calls=%fused_computation.151 | convolution fusion | flops 1572864 | bytes 4202496 | tf_op jit(solution)/shard_map/eval_jaxpr/tba,tb->ta/dot_general | solution.py:38
  100.6 2.3 %collective-permute-done.7 = f32[1,8,128]{2,1,0:T(8,128)S(1)} collective-permute-done((f32[1,8,128]{2,1,0:T(8,128)S(1)}, f32[1,8,128]{2,1,0:T(8,128)S(1)}, u32[]{:S(2)}, u32[]{:S(2)}) %collective-permute-start.7) | collective-permute-done | bytes 4128 | tf_op jit(solution)/shard_map/ppermute | solution.py:16
  103.1 1.6 %fusion.89 = f32[8,1,128]{2,1,0:T(1,128)S(1)} fusion(f32[64,128,128]{2,1,0:T(8,128)} %all-gather.4.cloned.1.call-done, f32[8,128,1]{1,2,0:T(1,128)S(1)} %bitcast.379), kind=kOutput, calls=%fused_computation.152 | convolution fusion | flops 1572864 | bytes 4202496 | tf_op jit(solution)/shard_map/eval_jaxpr/tba,tb->ta/dot_general | solution.py:38
  104.7 1.6 %fusion.90 = f32[8,1,128]{2,1,0:T(1,128)S(1)} fusion(f32[64,128,128]{2,1,0:T(8,128)} %all-gather.4.cloned.1.call-done, f32[8,128,1]{1,2,0:T(1,128)S(1)} %bitcast.374), kind=kOutput, calls=%fused_computation.153 | convolution fusion | flops 1572864 | bytes 4202496 | tf_op jit(solution)/shard_map/eval_jaxpr/tba,tb->ta/dot_general | solution.py:38
  (95 shorter events, 21.8 us)
Async XLA Ops:
  7.2 50.9 %all-gather.4.cloned.1.call-start = ((), (), s32[]{:S(2)}) async-start(), calls=%async_computation | async-start | bytes 4718592 | tf_op jit(solution)/shard_map/all_gather | solution.py:87
  8.0 3.2 %collective-permute-start = (f32[8,128]{1,0:T(8,128)S(1)}, f32[8,128]{1,0:T(8,128)S(1)}, u32[]{:S(2)}, u32[]{:S(2)}) collective-permute-start(f32[8,128]{1,0:T(8,128)S(1)} %slice_bitcast_fusion.12), channel_id=1, source_target_pairs={{0,4},{4,8},{8,12},{12,16},{16,20},{20,24},{24,28},{1,5},{5,9},{9,... | collective-permute-start | bytes 12296 | tf_op jit(solution)/shard_map/ppermute | solution.py:30
  11.9 4.8 %copy-start.2 = (f32[4,8,128,128]{3,2,1,0:T(8,128)S(1)}, f32[4,8,128,128]{3,2,1,0:T(8,128)}, u32[]{:S(2)}) copy-start(f32[4,8,128,128]{3,2,1,0:T(8,128)} %param.6) | copy-start | bytes 6291460
  11.9 5.7 %copy-start.3 = (f32[4,8,128]{2,1,0:T(8,128)S(1)}, f32[4,8,128]{2,1,0:T(8,128)}, u32[]{:S(2)}) copy-start(f32[4,8,128]{2,1,0:T(8,128)} %param.7) | copy-start | bytes 49156
  58.0 6.1 %copy-start = (f32[64,128,128]{2,1,0:T(8,128)S(1)}, f32[64,128,128]{2,1,0:T(8,128)}, u32[]{:S(2)}) copy-start(f32[64,128,128]{2,1,0:T(8,128)} %all-gather.4.cloned.1.call-done) | copy-start | bytes 12582916
  75.4 4.0 %collective-permute-start.1 = (f32[1,8,128]{2,1,0:T(8,128)S(1)}, f32[1,8,128]{2,1,0:T(8,128)S(1)}, u32[]{:S(2)}, u32[]{:S(2)}) collective-permute-start(f32[1,8,128]{2,1,0:T(8,128)S(1)} %multiply_bitcast_fusion), channel_id=1, source_target_pairs={{0,4},{4,8},{8,12},{12,16},{16,20},{20,24},{24,28},{28,0},{1,5},{5... | collective-permute-start | bytes 12296 | tf_op jit(solution)/shard_map/ppermute | solution.py:16
  79.4 3.9 %collective-permute-start.2 = (f32[1,8,128]{2,1,0:T(8,128)S(1)}, f32[1,8,128]{2,1,0:T(8,128)S(1)}, u32[]{:S(2)}, u32[]{:S(2)}) collective-permute-start(f32[1,8,128]{2,1,0:T(8,128)S(1)} %collective-permute-done.1), channel_id=1, source_target_pairs={{0,4},{4,8},{8,12},{12,16},{16,20},{20,24},{24,28},{28,0},{1,5},{5... | collective-permute-start | bytes 12296 | tf_op jit(solution)/shard_map/ppermute | solution.py:16
  83.3 3.9 %collective-permute-start.3 = (f32[1,8,128]{2,1,0:T(8,128)S(1)}, f32[1,8,128]{2,1,0:T(8,128)S(1)}, u32[]{:S(2)}, u32[]{:S(2)}) collective-permute-start(f32[1,8,128]{2,1,0:T(8,128)S(1)} %collective-permute-done.2), channel_id=1, source_target_pairs={{0,4},{4,8},{8,12},{12,16},{16,20},{20,24},{24,28},{28,0},{1,5},{5... | collective-permute-start | bytes 12296 | tf_op jit(solution)/shard_map/ppermute | solution.py:16
  87.2 3.9 %collective-permute-start.4 = (f32[1,8,128]{2,1,0:T(8,128)S(1)}, f32[1,8,128]{2,1,0:T(8,128)S(1)}, u32[]{:S(2)}, u32[]{:S(2)}) collective-permute-start(f32[1,8,128]{2,1,0:T(8,128)S(1)} %collective-permute-done.3), channel_id=1, source_target_pairs={{0,4},{4,8},{8,12},{12,16},{16,20},{20,24},{24,28},{28,0},{1,5},{5... | collective-permute-start | bytes 12296 | tf_op jit(solution)/shard_map/ppermute | solution.py:16
  91.2 3.9 %collective-permute-start.5 = (f32[1,8,128]{2,1,0:T(8,128)S(1)}, f32[1,8,128]{2,1,0:T(8,128)S(1)}, u32[]{:S(2)}, u32[]{:S(2)}) collective-permute-start(f32[1,8,128]{2,1,0:T(8,128)S(1)} %collective-permute-done.4), channel_id=1, source_target_pairs={{0,4},{4,8},{8,12},{12,16},{16,20},{20,24},{24,28},{28,0},{1,5},{5... | collective-permute-start | bytes 12296 | tf_op jit(solution)/shard_map/ppermute | solution.py:16
  95.1 3.9 %collective-permute-start.6 = (f32[1,8,128]{2,1,0:T(8,128)S(1)}, f32[1,8,128]{2,1,0:T(8,128)S(1)}, u32[]{:S(2)}, u32[]{:S(2)}) collective-permute-start(f32[1,8,128]{2,1,0:T(8,128)S(1)} %collective-permute-done.5), channel_id=1, source_target_pairs={{0,4},{4,8},{8,12},{12,16},{16,20},{20,24},{24,28},{28,0},{1,5},{5... | collective-permute-start | bytes 12296 | tf_op jit(solution)/shard_map/ppermute | solution.py:16
  95.1 11.2 %copy-start.1 = (f32[64,128,128]{2,1,0:T(8,128)S(1)}, f32[64,128,128]{2,1,0:T(8,128)}, u32[]{:S(2)}) copy-start(f32[64,128,128]{2,1,0:T(8,128)} %all-gather.4.cloned.1.call-done) | copy-start | bytes 12582916
  99.0 3.9 %collective-permute-start.7 = (f32[1,8,128]{2,1,0:T(8,128)S(1)}, f32[1,8,128]{2,1,0:T(8,128)S(1)}, u32[]{:S(2)}, u32[]{:S(2)}) collective-permute-start(f32[1,8,128]{2,1,0:T(8,128)S(1)} %collective-permute-done.6), channel_id=1, source_target_pairs={{0,4},{4,8},{8,12},{12,16},{16,20},{20,24},{24,28},{28,0},{1,5},{5... | collective-permute-start | bytes 12296 | tf_op jit(solution)/shard_map/ppermute | solution.py:16
  106.9 6.1 %copy-start.4 = (s32[4,8,128]{2,1,0:T(8,128)S(1)}, s32[4,8,128]{2,1,0:T(8,128)}, u32[]{:S(2)}) copy-start(s32[4,8,128]{2,1,0:T(8,128)} %param.10) | copy-start | bytes 49156
Sparse Core Ops, SparseCore 0:
  16.8 41.1 all-gather.3
